TPU v7x, 32 devices: a whole 2x2x4 slice. The times are simulated.
32 devices in a mesh: tiles: 2 (over y), strip: 4 (over z), col: 2 (over x), expo: 2 (over core).
Axes of the slice: x: 2, y: 2, z: 4, core: 2. Of those that a mesh axis runs over, the one named last changes fastest.
Arguments:
- mask_params: float32 [2, 2048, 256], P('expo', ('tiles', 'strip'), 'col'), parts along dimension 1, may hold values from -3 to 3
- target: int32 [2048, 256], P(('tiles', 'strip'), 'col'), parts along dimension 0, may hold values from 0 to 1, as said below
- col_taps: bfloat16 [24, 2, 65], replicated, may hold values from -0.75 to 0.75
- row_taps: bfloat16 [24, 2, 65], replicated, may hold values from -0.75 to 0.75
- kernel_weights: float32 [24], replicated, may hold values from 0.05 to 0.5
Outputs:
- new_params: float32 [2, 2048, 256], P('expo', ('tiles', 'strip'), 'col'), parts along dimension 1
- resist: float32 [2048, 256], P(('tiles', 'strip'), 'col'), parts along dimension 0
- mean_loss: float32 [2], P('tiles'), parts along dimension 0
There are 2 independent parts, one for each index of `tiles`. A program takes and returns all parts, laid end to end along the dimension named above; an argument that names none is the same for every part. Nothing has to cross between parts.
Inputs may be any that keep to these rules, and one draw needn't show every extreme that they name: `target`: 1 where the layout is printed, 0 elsewhere.
All inputs are finite; a program needn't handle non-finite values.
Results may differ from a plain program's by a relative error of at most 0.0078.
Values may be sent and summed in bfloat16 or wider, within the bound.
No kernel may reach another device: no remote copies, remote signals or barrier semaphores. Data moves between devices by JAX's collectives and lax.ppermute only.
A program may use at most 64 MiB of HBM per device.

v0:
```python
import jax
import jax.numpy as jnp
from jax import lax
from jax.sharding import PartitionSpec as P

HALF = 32
mask_slope = 4.0
resist_steep = 4.0
resist_level = 3.0
step_length = 0.5
norm_eps = 1e-06


def extended(array, sides, width):
    for axis, dim in sides:
        peers, length = (lax.axis_size(axis), array.shape[dim])
        up = [(i, (i + 1) % peers) for i in range(peers - 1)]
        down = [(j, i) for i, j in up]
        last = lax.slice_in_dim(array, length - width, length, axis=dim)
        first = lax.slice_in_dim(array, 0, width, axis=dim)
        before = lax.ppermute(last, axis, up)
        after = lax.ppermute(first, axis, down)
        array = jnp.concatenate([before, array, after], axis=dim)
    return array


def block_size():
    return 128


def toeplitz(tap_values, block_len):
    tap_count = tap_values.shape[-1]
    window_len = block_len + tap_count - 1
    padded_taps = jnp.concatenate(
        [tap_values, jnp.zeros(tap_values.shape[:-1] + (block_len,), tap_values.dtype)], axis=-1
    )
    repeated = jnp.tile(padded_taps, (1,) * (tap_values.ndim - 1) + (block_len,))
    return repeated[..., : block_len * window_len].reshape(
        tap_values.shape[:-1] + (block_len, window_len)
    )


def col_pass(source, tap_table):
    block_len, window_len = (tap_table.shape[1], tap_table.shape[2])
    length = source.shape[-1] - window_len + block_len
    windows = jnp.stack([source], axis=1)
    result = jnp.einsum("rnw,pow->prno", windows, tap_table, preferred_element_type=jnp.float32)
    return result.reshape(tap_table.shape[0], source.shape[0], length)


def row_pass(source, tap_table):
    block_len, window_len = (tap_table.shape[1], tap_table.shape[2])
    length = source.shape[1] - window_len + block_len
    windows = jnp.stack(
        [
            source[:, offset * block_len : offset * block_len + window_len, :]
            for offset in range(length // block_len)
        ],
        axis=1,
    )
    result = jnp.einsum("pnwc,qow->pqnoc", windows, tap_table, preferred_element_type=jnp.float32)
    return result.reshape(source.shape[0], tap_table.shape[0], length, source.shape[2])


def col_adjoint(source, tap_table):
    block_len, window_len = (tap_table.shape[1], tap_table.shape[2])
    length = source.shape[-1] - window_len + block_len
    windows = jnp.stack([source], axis=2)
    result = jnp.einsum("prnw,pow->rno", windows, tap_table, preferred_element_type=jnp.float32)
    return result.reshape(source.shape[1], length)


def shards(mask_params, target, col_taps, row_taps, kernel_weights):
    row_count, col_count = target.shape
    mask_field = jax.nn.sigmoid(mask_slope * mask_params[0])
    mask_half = mask_field.astype(jnp.bfloat16)
    col_block = block_size()
    row_block = block_size()
    mask_ext = extended(mask_half, (("strip", 0), ("col", 1)), HALF)

    def add_intensity(running, kernel):
        col_pair = col_taps[kernel]
        row_pair = row_taps[kernel]
        columns = col_pass(mask_ext, toeplitz(col_pair, col_block)).astype(jnp.bfloat16)
        pair_sums = row_pass(columns, toeplitz(row_pair, row_block))
        real_part = pair_sums[0, 0] - pair_sums[1, 1]
        imag_part = pair_sums[0, 1] + pair_sums[1, 0]
        updated = running + kernel_weights[kernel] * (real_part * real_part + imag_part * imag_part)
        return (updated, (real_part, imag_part))

    kernel_ids = jnp.arange(kernel_weights.shape[0], dtype=jnp.int32)
    zero_field = jnp.zeros((row_count, col_count), jnp.float32)
    intensity, stored = lax.scan(add_intensity, zero_field, kernel_ids)
    summed = lax.psum(intensity, "expo")
    resist = jax.nn.sigmoid(resist_steep * (summed - resist_level))
    mismatch = resist - target.astype(jnp.float32)
    pixels = row_count * col_count * lax.axis_size("strip") * lax.axis_size("col")
    loss_local = jnp.sum(mismatch * mismatch)
    loss_sum = lax.psum(loss_local, ("strip", "col"))
    slope_field = 2.0 * mismatch * resist_steep * resist * (1.0 - resist)

    def add_gradient(running, inputs):
        kernel, real_part, imag_part = inputs
        col_pair = col_taps[kernel]
        row_pair = row_taps[kernel]
        weighting = 2.0 * kernel_weights[kernel] * slope_field
        products = jnp.stack([weighting * real_part, weighting * imag_part]).astype(jnp.bfloat16)
        product_ext = extended(products, (("strip", 1),), HALF)
        returned = row_pass(product_ext, toeplitz(row_pair[:, ::-1], row_block))
        unrolled = jnp.stack(
            [returned[0, 0] + returned[1, 1], returned[1, 0] - returned[0, 1]]
        ).astype(jnp.bfloat16)
        unrolled_ext = extended(unrolled, (("col", 2),), HALF)
        return (running + col_adjoint(unrolled_ext, toeplitz(col_pair[:, ::-1], col_block)), None)

    descent, unused = lax.scan(add_gradient, zero_field, (kernel_ids, stored[0], stored[1]))
    gradient = descent * mask_slope * mask_field * (1.0 - mask_field)
    grad_squares = jnp.sum(gradient * gradient)
    square_sum = lax.psum(grad_squares, ("strip", "col", "expo"))
    root_mean = jnp.sqrt(square_sum / (lax.axis_size("expo") * pixels) + norm_eps)
    new_params = mask_params - step_length * gradient[None] / root_mean
    mean_loss = (loss_sum / pixels).reshape(1)
    return (new_params, resist, mean_loss)


def solution(mesh):
    return jax.shard_map(
        shards,
        mesh=mesh,
        in_specs=(
            P("expo", ("tiles", "strip"), "col"),
            P(("tiles", "strip"), "col"),
            P(),
            P(),
            P(),
        ),
        out_specs=(P("expo", ("tiles", "strip"), "col"), P(("tiles", "strip"), "col"), P("tiles")),
        check_vma=False,
    )
```

profile of v0, /device:TPU:0, one launch (start us, length us, event | category | flops | bytes accessed | tf_op | source)
XLA Modules:
  0.0 801.6 jit_solution(15718260283883890776)
XLA Ops:
  8.2 5.0 collective-permute-start.4
  14.5 4.2 collective-permute-done.5
  18.8 3.4 collective-permute-start.6
  24.2 4.3 collective-permute-done.7
  28.8 172.5 %while.26 = (s32[]{:T(128)}, f32[256,128]{1,0:T(8,128)S(1)}, f32[24,256,128]{2,1,0:T(8,128)}, f32[24,256,128]{2,1,0:T(8,128)}, s32[24]{0:T(128)S(1)}, /*index=5*...) while((s32[]{:T(128)}, f32[256,128]{1,0:T(8,128)S(1)}, ...), condition=%wide.region_1.2_spmd.clone, body=%wide.region_0.1_spmd.clone.sunk | while | flops 82296832 | bytes 4555409 | solution.py:93
  202.0 17.4 %all-reduce.6.cloned.1.call-done = f32[256,128]{1,0:T(8,128)} async-done(((f32[256,128]{1,0:T(8,128)}), f32[256,128]{1,0:T(8,128)}) %all-reduce.6.cloned.1.call-update) | async-done | bytes 131088 | tf_op jit(solution)/shard_map/psum | solution.py:94
  221.7 521.3 %while.27 = (s32[]{:T(128)}, f32[256,128]{1,0:T(8,128)S(1)}, s32[24]{0:T(128)S(1)}, bf16[24,2,65]{2,1,0:T(2,128)(2,1)}, f32[24]{0:T(128)}, /*index=5*/f32[256,12...) while((s32[]{:T(128)}, f32[256,128]{1,0:T(8,128)S(1)}, ...), condition=%wide.region_4.5_spmd.clone, body=%wide.region_3.4_spmd.clone.sunk | while | flops 77824000 | bytes 7152573 | solution.py:116
  227.1 3.7 collective-permute-start
  233.6 2.9 collective-permute-done.1
  238.5 4.5 collective-permute-start.3
  250.4 3.4 collective-permute-start
  256.6 2.9 collective-permute-done.1
  261.5 4.5 collective-permute-start.3
  273.4 3.4 collective-permute-start
  284.5 4.5 collective-permute-start.3
  301.1 2.9 collective-permute-done.1
  306.0 4.5 collective-permute-start.3
  322.6 2.9 collective-permute-done.1
  327.5 4.5 collective-permute-start.3
  344.1 2.9 collective-permute-done.1
  349.0 4.5 collective-permute-start.3
  365.6 2.9 collective-permute-done.1
  370.5 4.5 collective-permute-start.3
  387.1 2.9 collective-permute-done.1
  392.1 4.5 collective-permute-start.3
  408.6 2.9 collective-permute-done.1
  413.6 4.5 collective-permute-start.3
  430.2 2.9 collective-permute-done.1
  435.1 4.5 collective-permute-start.3
  451.7 2.9 collective-permute-done.1
  456.6 4.5 collective-permute-start.3
  473.4 2.9 collective-permute-done.1
  478.3 4.5 collective-permute-start.3
  494.9 2.9 collective-permute-done.1
  499.8 4.5 collective-permute-start.3
  521.3 4.5 collective-permute-start.3
  542.8 4.5 collective-permute-start.3
  564.3 4.5 collective-permute-start.3
  585.8 4.5 collective-permute-start.3
  607.4 4.5 collective-permute-start.3
  628.9 4.5 collective-permute-start.3
  650.4 4.5 collective-permute-start.3
  672.0 4.5 collective-permute-start.3
  693.5 4.5 collective-permute-start.3
  715.0 4.5 collective-permute-start.3
  736.6 4.5 collective-permute-start.3
  743.7 30.1 %psum.22 = f32[]{:T(128)} all-reduce(f32[]{:T(128)} %multiply_reduce_fusion.1), channel_id=1, replica_groups=mesh['tiles'=2,'strip'=4,'col'=2,'expo'=2] {'strip','col','expo'}, use_global_device_ids=true, to_apply=%region_6.7 | all-reduce | flops 1 | bytes 8 | tf_op jit(solution)/shard_map/psum | solution.py:119
  775.2 17.7 %psum.23 = f32[]{:T(128)} all-reduce(f32[]{:T(128)} %get-tuple-element.217), channel_id=1, replica_groups=mesh['tiles'=2,'strip'=4,'col'=2,'expo'=2] {'strip','col'}, use_global_device_ids=true, to_apply=%region_8.9 | all-reduce | flops 1 | bytes 8 | tf_op jit(solution)/shard_map/psum | solution.py:99
  (1335 shorter events, 433.0 us)
Async XLA Ops:
  7.2 212.2 %all-reduce.6.cloned.1.call-start = ((), (), s32[]{:S(2)}) async-start(), calls=%async_computation | async-start | bytes 262144 | tf_op jit(solution)/shard_map/psum | solution.py:94
  8.2 6.3 collective-permute-start.4
  22.2 6.3 collective-permute-start.7
  227.1 6.5 collective-permute-start
  237.2 6.6 collective-permute-start.2
  238.5 6.1 collective-permute-start.3
  250.4 6.2 collective-permute-start
  260.2 6.6 collective-permute-start.2
  261.5 6.1 collective-permute-start.3
  273.4 6.2 collective-permute-start
  283.2 6.6 collective-permute-start.2
  284.5 6.1 collective-permute-start.3
  304.7 6.6 collective-permute-start.2
  306.0 6.1 collective-permute-start.3
  326.2 6.6 collective-permute-start.2
  327.5 6.1 collective-permute-start.3
  347.7 6.6 collective-permute-start.2
  349.0 6.1 collective-permute-start.3
  369.2 6.6 collective-permute-start.2
  370.5 6.1 collective-permute-start.3
  390.8 6.6 collective-permute-start.2
  392.1 6.1 collective-permute-start.3
  412.3 6.6 collective-permute-start.2
  413.6 6.1 collective-permute-start.3
  433.8 6.6 collective-permute-start.2
  435.1 6.1 collective-permute-start.3
  455.3 6.6 collective-permute-start.2
  456.6 6.1 collective-permute-start.3
  477.0 6.6 collective-permute-start.2
  478.3 6.1 collective-permute-start.3
  498.5 6.6 collective-permute-start.2
  499.8 6.1 collective-permute-start.3
  520.0 6.6 collective-permute-start.2
  521.3 6.1 collective-permute-start.3
  541.5 6.6 collective-permute-start.2
  542.8 6.1 collective-permute-start.3
  563.0 6.6 collective-permute-start.2
  564.3 6.1 collective-permute-start.3
  584.5 6.6 collective-permute-start.2
  585.8 6.1 collective-permute-start.3
  606.1 6.6 collective-permute-start.2
  607.4 6.1 collective-permute-start.3
  627.6 6.6 collective-permute-start.2
  649.1 6.6 collective-permute-start.2
  670.7 6.6 collective-permute-start.2
  692.2 6.6 collective-permute-start.2
  713.8 6.6 collective-permute-start.2
  735.3 6.6 collective-permute-start.2
  (81 other events, 1135.7 us)
Sparse Core Ops, SparseCore 0:
  202.1 17.2 all-reduce.5
where the time goes:
time: 807 us; the launch traced here: 802 us
  starting transfers between devices  233 us (29%)
  local copies, waits for them, and re-layouts  185 us (23%)
  loops' own time  116 us (14%)
  waiting for transfers between devices  114 us (14%)
  other arithmetic  65.4 us (8%)
  blocking collectives  47.8 us (6%)
  matrix products  23.3 us (3%)
  between operations  16.7 us (2%)
    ppermute x50, starting transfers between devices, extended(): before = lax.ppermute(last, axis, up)  169 us
    ppermute x50, waiting for transfers between devices, extended(): after = lax.ppermute(first, axis, down)  77.3 us
    another operation x1, loops' own time, shards(): lax.scan(add_gradient, zero_field, (kernel_ids, stored[0], stored[1]))  67 us
    ppermute x50, starting transfers between devices, extended(): after = lax.ppermute(first, axis, down)  64.6 us
    another operation x1, loops' own time, shards(): intensity, stored = lax.scan(add_intensity, zero_field, kernel_ids)  48.9 us
    another operation x192, local copies, waits for them, and re-layouts, toeplitz(): jnp.tile(padded_taps, (1,) * (tap_values.ndim - 1) + (block_len,))  42.5 us
    psum x1, blocking collectives, shards(): square_sum = lax.psum(grad_squares, ('strip', 'col', 'expo'))  30.1 us
    dynamic_slice x24, local copies, waits for them, and re-layouts, add_gradient(): weighting = 2.0 * kernel_weights[kernel] * slope_field  29.8 us
  transfers between devices with their start and end apart: 101, of which 52 were waited for; matrix products, arithmetic and copies ran while one was open for 7% of the time, Pallas kernels for 0%

commit v1 on v0

--- a/solution.py
+++ b/solution.py
@@ -1,3 +1,4 @@
+import functools
 import jax
 import jax.numpy as jnp
 from jax import lax
@@ -9,6 +10,14 @@
 resist_level = 3.0
 step_length = 0.5
 norm_eps = 1e-06
+
+
+def close_signs_now(t0, mesh_name):
+    b_next = jax.lax.all_gather(t0, mesh_name)
+    return jnp.sum(b_next, axis=0)
+
+
+state_zone_on_mesh = functools.partial(close_signs_now, mesh_name="expo")
 
 
 def extended(array, sides, width):
@@ -91,7 +100,7 @@
     kernel_ids = jnp.arange(kernel_weights.shape[0], dtype=jnp.int32)
     zero_field = jnp.zeros((row_count, col_count), jnp.float32)
     intensity, stored = lax.scan(add_intensity, zero_field, kernel_ids)
-    summed = lax.psum(intensity, "expo")
+    summed = state_zone_on_mesh(intensity)
     resist = jax.nn.sigmoid(resist_steep * (summed - resist_level))
     mismatch = resist - target.astype(jnp.float32)
     pixels = row_count * col_count * lax.axis_size("strip") * lax.axis_size("col")

time: 807 us -> 775 us (0.960)
  waiting for transfers between devices: 114 us -> 96.9 us
  between operations: 16.7 us -> 3.26 us
    psum x1 -> x0, waiting for transfers between devices: 17.4 us -> none  [shards(): summed = lax.psum(intensity, 'expo')]
  transfers between devices with their start and end apart: 101 -> 100, of which waited for: 52 -> 51; matrix products, arithmetic and copies ran while one was open for 7% -> 7% of each run, Pallas kernels for 0% -> 0%
where the time goes in v1:
time: 775 us; the launch traced here: 769 us
  starting transfers between devices  231 us (30%)
  local copies, waits for them, and re-layouts  184 us (24%)
  loops' own time  116 us (15%)
  waiting for transfers between devices  96.9 us (13%)
  other arithmetic  64.5 us (8%)
  blocking collectives  49.8 us (6%)
  matrix products  23.3 us (3%)
    ppermute x50, starting transfers between devices, extended(): before = lax.ppermute(last, axis, up)  167 us
    ppermute x50, waiting for transfers between devices, extended(): after = lax.ppermute(first, axis, down)  77.3 us
    another operation x1, loops' own time, shards(): lax.scan(add_gradient, zero_field, (kernel_ids, stored[0], stored[1]))  67 us
    ppermute x50, starting transfers between devices, extended(): after = lax.ppermute(first, axis, down)  64.6 us
    another operation x1, loops' own time, shards(): intensity, stored = lax.scan(add_intensity, zero_field, kernel_ids)  48.9 us
    another operation x192, local copies, waits for them, and re-layouts, toeplitz(): jnp.tile(padded_taps, (1,) * (tap_values.ndim - 1) + (block_len,))  42.5 us
    psum x1, blocking collectives, shards(): square_sum = lax.psum(grad_squares, ('strip', 'col', 'expo'))  30.1 us
    dynamic_slice x24, local copies, waits for them, and re-layouts, add_gradient(): weighting = 2.0 * kernel_weights[kernel] * slope_field  29.8 us
  transfers between devices with their start and end apart: 100, of which 51 were waited for; matrix products, arithmetic and copies ran while one was open for 7% of the time, Pallas kernels for 0%

profile of v1, /device:TPU:0, one launch (start us, length us, event | category | flops | bytes accessed | tf_op | source)
XLA Modules:
  0.0 769.4 jit_solution(14577342088156956495)
XLA Ops:
  1.6 5.0 collective-permute-start.4
  7.9 4.2 collective-permute-done.5
  12.2 3.4 collective-permute-start.6
  17.7 4.3 collective-permute-done.7
  22.3 172.4 %while.26 = (s32[]{:T(128)}, f32[256,128]{1,0:T(8,128)S(1)}, f32[24,256,128]{2,1,0:T(8,128)}, f32[24,256,128]{2,1,0:T(8,128)}, s32[24]{0:T(128)S(1)}, /*index=5*...) while((s32[]{:T(128)}, f32[256,128]{1,0:T(8,128)S(1)}, ...), condition=%wide.region_1.2_spmd.clone, body=%wide.region_0.1_spmd.clone.sunk | while | flops 82296832 | bytes 4555409 | solution.py:102
  198.1 519.5 %while.27 = (s32[]{:T(128)}, f32[256,128]{1,0:T(8,128)S(1)}, s32[24]{0:T(128)S(1)}, bf16[24,2,65]{2,1,0:T(2,128)(2,1)}, f32[24]{0:T(128)}, /*index=5*/f32[256,12...) while((s32[]{:T(128)}, f32[256,128]{1,0:T(8,128)S(1)}, ...), condition=%wide.region_4.5_spmd.clone, body=%wide.region_3.4_spmd.clone.sunk | while | flops 77824000 | bytes 7152573 | solution.py:125
  203.6 3.5 collective-permute-start
  209.8 2.9 collective-permute-done.1
  214.7 4.5 collective-permute-start.3
  226.6 3.5 collective-permute-start
  232.9 2.9 collective-permute-done.1
  237.8 4.5 collective-permute-start.3
  254.4 2.9 collective-permute-done.1
  259.3 4.5 collective-permute-start.3
  275.9 2.9 collective-permute-done.1
  280.8 4.5 collective-permute-start.3
  297.4 2.9 collective-permute-done.1
  302.4 4.5 collective-permute-start.3
  318.9 2.9 collective-permute-done.1
  323.9 4.5 collective-permute-start.3
  340.4 2.9 collective-permute-done.1
  345.4 4.5 collective-permute-start.3
  366.9 4.5 collective-permute-start.3
  388.4 4.5 collective-permute-start.3
  405.0 2.9 collective-permute-done.1
  409.9 4.5 collective-permute-start.3
  426.6 2.9 collective-permute-done.1
  431.5 4.5 collective-permute-start.3
  448.1 2.9 collective-permute-done.1
  453.0 4.5 collective-permute-start.3
  469.6 2.9 collective-permute-done.1
  474.5 4.5 collective-permute-start.3
  491.1 2.9 collective-permute-done.1
  496.0 4.5 collective-permute-start.3
  512.6 2.9 collective-permute-done.1
  517.6 4.5 collective-permute-start.3
  534.1 2.9 collective-permute-done.1
  539.1 4.5 collective-permute-start.3
  560.6 4.5 collective-permute-start.3
  582.1 4.5 collective-permute-start.3
  603.6 4.5 collective-permute-start.3
  625.1 4.5 collective-permute-start.3
  646.6 4.5 collective-permute-start.3
  668.2 4.5 collective-permute-start.3
  689.7 4.5 collective-permute-start.3
  711.2 4.5 collective-permute-start.3
  718.3 30.1 %psum.14 = f32[]{:T(128)} all-reduce(f32[]{:T(128)} %multiply_reduce_fusion.1), channel_id=1, replica_groups=mesh['tiles'=2,'strip'=4,'col'=2,'expo'=2] {'strip','col','expo'}, use_global_device_ids=true, to_apply=%region_6.7 | all-reduce | flops 1 | bytes 8 | tf_op jit(solution)/shard_map/psum | solution.py:128
  749.8 17.7 %psum.15 = f32[]{:T(128)} all-reduce(f32[]{:T(128)} %get-tuple-element.217), channel_id=1, replica_groups=mesh['tiles'=2,'strip'=4,'col'=2,'expo'=2] {'strip','col'}, use_global_device_ids=true, to_apply=%region_8.9 | all-reduce | flops 1 | bytes 8 | tf_op jit(solution)/shard_map/psum | solution.py:108
  (1332 shorter events, 429.3 us)
Async XLA Ops:
  1.6 6.3 collective-permute-start.4
  15.6 6.3 collective-permute-start.7
  203.6 6.3 collective-permute-start
  213.4 6.6 collective-permute-start.2
  214.7 6.1 collective-permute-start.3
  226.6 6.2 collective-permute-start
  236.5 6.6 collective-permute-start.2
  237.8 6.1 collective-permute-start.3
  258.0 6.6 collective-permute-start.2
  259.3 6.1 collective-permute-start.3
  279.5 6.6 collective-permute-start.2
  301.1 6.6 collective-permute-start.2
  302.4 6.1 collective-permute-start.3
  322.6 6.6 collective-permute-start.2
  323.9 6.1 collective-permute-start.3
  344.1 6.6 collective-permute-start.2
  345.4 6.1 collective-permute-start.3
  365.6 6.6 collective-permute-start.2
  366.9 6.1 collective-permute-start.3
  387.1 6.6 collective-permute-start.2
  388.4 6.1 collective-permute-start.3
  408.6 6.6 collective-permute-start.2
  409.9 6.1 collective-permute-start.3
  430.2 6.6 collective-permute-start.2
  431.5 6.1 collective-permute-start.3
  451.7 6.6 collective-permute-start.2
  453.0 6.1 collective-permute-start.3
  473.2 6.6 collective-permute-start.2
  474.5 6.1 collective-permute-start.3
  494.7 6.6 collective-permute-start.2
  496.0 6.1 collective-permute-start.3
  516.3 6.6 collective-permute-start.2
  517.6 6.1 collective-permute-start.3
  537.8 6.6 collective-permute-start.2
  539.1 6.1 collective-permute-start.3
  559.3 6.6 collective-permute-start.2
  560.6 6.1 collective-permute-start.3
  580.8 6.6 collective-permute-start.2
  582.1 6.1 collective-permute-start.3
  602.3 6.6 collective-permute-start.2
  603.6 6.1 collective-permute-start.3
  623.8 6.6 collective-permute-start.2
  625.1 6.1 collective-permute-start.3
  645.3 6.6 collective-permute-start.2
  646.6 6.1 collective-permute-start.3
  666.9 6.6 collective-permute-start.2
  688.4 6.6 collective-permute-start.2
  709.9 6.6 collective-permute-start.2
  (79 other events, 1109.4 us)
